TPU v7x, 32 devices: a whole 2x2x4 slice. The times are simulated.
32 devices in a mesh: fsdp: 8 (over z, x), tp: 4 (over y, core).
Axes of the slice: x: 2, y: 2, z: 4, core: 2. Of those that a mesh axis runs over, the one named last changes fastest.
Arguments:
- tokens: bfloat16 [1024, 4096], P('fsdp'), may hold values from -6 to 6
- gate_left: bfloat16 [4096, 1024], P('fsdp', 'tp'), may hold values from -0.09375 to 0.09375
- gate_right: bfloat16 [1024, 14336], P('fsdp', 'tp'), may hold values from -0.1875 to 0.1875
- gate_values: bfloat16 [108, 16384], P('tp', 'fsdp'), may hold values from -0.5 to 0.5
- gate_rows: int32 [108], P('tp'), may hold values from 0 to 31
- gate_cols: int32 [108], P('tp'), may hold values from 0 to 111, as said below
- up_left: bfloat16 [4096, 1024], P('fsdp', 'tp'), may hold values from -0.09375 to 0.09375
- up_right: bfloat16 [1024, 14336], P('fsdp', 'tp'), may hold values from -0.1875 to 0.1875
- up_values: bfloat16 [108, 16384], P('tp', 'fsdp'), may hold values from -0.5 to 0.5
- up_rows: int32 [108], P('tp'), may hold values from 0 to 31
- up_cols: int32 [108], P('tp'), may hold values from 0 to 111, as said below
- grad_hidden: bfloat16 [1024, 14336], P('fsdp', 'tp'), may hold values from -6 to 6
Outputs:
- hidden: bfloat16 [1024, 14336], P('fsdp', 'tp')
- grad_gate_values: float32 [108, 16384], P('tp', 'fsdp')
- grad_up_values: float32 [108, 16384], P('tp', 'fsdp')
Inputs may be any that keep to these rules, and one draw needn't show every extreme that they name: `gate_cols`: support blocks of one projection are distinct (row block, column block) pairs; the entries that lie on index t of tp have column blocks from t * 14336 // (128 * 4) to (t + 1) * 14336 // (128 * 4) - 1. Rows and columns of one projection go together. `up_cols`: as for the gate projection.
All inputs are finite; a program needn't handle non-finite values.
Results may differ from a plain program's by a relative error of at most 0.005.
Values may be sent and summed in bfloat16 or wider, within the bound.
No kernel may reach another device: no remote copies, remote signals or barrier semaphores. Data moves between devices by JAX's collectives and lax.ppermute only.
A program may use at most 128 MiB of HBM per device.

v0:
```python
import jax
import jax.numpy as jnp
from jax import lax
from jax.sharding import PartitionSpec as P

BLK = 128


def support_forward(tokens, blocks, rows, cols_local, col_blocks):
    width = tokens.shape[1] // BLK
    sources = tokens.reshape(tokens.shape[0], width, BLK)[:, rows, :]
    parts = jnp.einsum("tkb,kbc->tkc", sources, blocks, preferred_element_type=jnp.float32)
    placed = (
        jnp.zeros((tokens.shape[0], col_blocks, BLK), jnp.float32).at[:, cols_local, :].add(parts)
    )
    return (placed.reshape(tokens.shape[0], col_blocks * BLK), sources)


def value_terms(sources_gate, dpre_gate, local_gate, sources_up, dpre_up, local_up, col_blocks):
    picked_gate = dpre_gate.reshape(dpre_gate.shape[0], col_blocks, BLK)[:, local_gate, :]
    picked_up = dpre_up.reshape(dpre_up.shape[0], col_blocks, BLK)[:, local_up, :]
    value_gate = jnp.einsum(
        "tkb,tkc->kbc", sources_gate, picked_gate, preferred_element_type=jnp.float32
    )
    value_up = jnp.einsum("tkb,tkc->kbc", sources_up, picked_up, preferred_element_type=jnp.float32)
    return (
        value_gate.reshape(value_gate.shape[0], BLK * BLK),
        value_up.reshape(value_up.shape[0], BLK * BLK),
    )


def on_device(
    tokens,
    gate_left,
    gate_right,
    gate_values,
    gate_rows,
    gate_cols,
    up_left,
    up_right,
    up_values,
    up_rows,
    up_cols,
    grad_hidden,
):
    left_gate, left_up = (
        lax.all_gather(gate_left, "fsdp", axis=0, tiled=True),
        lax.all_gather(up_left, "fsdp", axis=0, tiled=True),
    )
    rank_gate = jnp.dot(tokens, left_gate, preferred_element_type=jnp.float32).astype(jnp.bfloat16)
    rank_up = jnp.dot(tokens, left_up, preferred_element_type=jnp.float32).astype(jnp.bfloat16)
    full_gate, full_up = (
        lax.all_gather(rank_gate, "tp", axis=1, tiled=True),
        lax.all_gather(rank_up, "tp", axis=1, tiled=True),
    )
    flat_gate, flat_up = (
        lax.all_gather(gate_values, "fsdp", axis=1, tiled=True),
        lax.all_gather(up_values, "fsdp", axis=1, tiled=True),
    )
    blocks_gate = flat_gate.reshape(flat_gate.shape[0], BLK, BLK)
    blocks_up = flat_up.reshape(flat_up.shape[0], BLK, BLK)
    right_gate = lax.all_gather(gate_right, "fsdp", axis=0, tiled=True)
    right_up = lax.all_gather(up_right, "fsdp", axis=0, tiled=True)
    col_blocks = right_gate.shape[1] // BLK
    col_base = lax.axis_index("tp") * col_blocks
    local_gate = gate_cols - col_base
    local_up = up_cols - col_base
    sparse_gate, sources_gate = support_forward(
        tokens, blocks_gate, gate_rows, local_gate, col_blocks
    )
    sparse_up, sources_up = support_forward(tokens, blocks_up, up_rows, local_up, col_blocks)
    pre_gate = jnp.dot(full_gate, right_gate, preferred_element_type=jnp.float32) + sparse_gate
    pre_up = jnp.dot(full_up, right_up, preferred_element_type=jnp.float32) + sparse_up
    sigma = jax.nn.sigmoid(pre_gate)
    silu = pre_gate * sigma
    upstream = grad_hidden.astype(jnp.float32)
    dpre_gate = (upstream * pre_up * sigma * (1.0 + pre_gate * (1.0 - sigma))).astype(jnp.bfloat16)
    dpre_up = (upstream * silu).astype(jnp.bfloat16)
    hidden = (silu * pre_up).astype(jnp.bfloat16)
    value_gate, value_up = value_terms(
        sources_gate, dpre_gate, local_gate, sources_up, dpre_up, local_up, col_blocks
    )
    grad_gate_values, grad_up_values = (
        lax.psum_scatter(value_gate, "fsdp", scatter_dimension=1, tiled=True),
        lax.psum_scatter(value_up, "fsdp", scatter_dimension=1, tiled=True),
    )
    return (hidden, grad_gate_values, grad_up_values)


def solution(mesh):
    return jax.shard_map(
        on_device,
        mesh=mesh,
        in_specs=(
            P("fsdp", None),
            P("fsdp", "tp"),
            P("fsdp", "tp"),
            P("tp", "fsdp"),
            P("tp"),
            P("tp"),
            P("fsdp", "tp"),
            P("fsdp", "tp"),
            P("tp", "fsdp"),
            P("tp"),
            P("tp"),
            P("fsdp", "tp"),
        ),
        out_specs=(P("fsdp", "tp"), P("tp", "fsdp"), P("tp", "fsdp")),
        check_vma=False,
    )
```

profile of v0, /device:TPU:0, one launch (start us, length us, event | category | flops | bytes accessed | tf_op | source)
XLA Modules:
  0.0 506.7 jit_solution(9324583249922640998)
XLA Ops:
  7.2 0.0 copy-start
  7.2 0.0 all-gather.5.cloned.1.call-start
  7.2 0.7 all-gather.5.cloned.1.call-update
  7.9 0.0 all-gather.9.cloned.1.call-start
  8.0 0.7 all-gather.9.cloned.1.call-update
  8.7 0.0 all-gather.7.cloned.1.call-start
  8.7 0.7 all-gather.7.cloned.1.call-update
  9.4 0.0 all-gather.11.cloned.1.call-start
  9.4 0.5 all-gather.11.cloned.1.call-update
  10.0 0.0 reduce-scatter.5.cloned.1.call-start
  10.0 0.0 copy-done
  10.0 0.0 copy-start.9
  10.0 0.7 copy.29
  10.7 0.7 copy.30
  11.4 0.0 copy-done.9
  11.4 0.0 copy-start.1
  11.4 0.0 copy-start.13
  11.4 36.4 %all_gather.27 = bf16[27,16384]{1,0:T(8,128)(2,1)S(1)} all-gather(bf16[27,2048]{1,0:T(8,128)(2,1)S(1)} %copy-done.9), channel_id=1, replica_groups=mesh['fsdp'=8,'tp'=4] {'fsdp'}, dimensions={1}, use_global_device_ids=true | all-gather | bytes 995328 | tf_op jit(solution)/shard_map/all_gather | solution.py:57
  47.8 1.2 copy.44
  49.0 0.7 gather_fusion
  49.8 3.1 fusion.7
  52.9 0.2 broadcast.15.clone
  53.1 4.6 scatter_fusion
  57.7 1.7 copy.31
  59.4 2.8 copy.32
  62.2 0.7 gather_fusion.1
  63.0 0.1 copy-done.10
  63.1 36.5 %all_gather.31 = bf16[27,16384]{1,0:T(8,128)(2,1)S(1)} all-gather(bf16[27,2048]{1,0:T(8,128)(2,1)S(1)} %copy-done.10), channel_id=1, replica_groups=mesh['fsdp'=8,'tp'=4] {'fsdp'}, dimensions={1}, use_global_device_ids=true | all-gather | bytes 995328 | tf_op jit(solution)/shard_map/all_gather | solution.py:58
  99.6 0.2 copy.45
  99.8 1.7 fusion.5
  101.5 0.0 copy-done.5
  101.5 0.2 broadcast.15.clone.1
  101.7 4.6 scatter_fusion.1
  106.3 1.7 copy.34
  107.9 2.8 copy.35
  110.7 0.0 all-gather.5.cloned.1.call-done
  110.7 2.0 convolution_convert_fusion.1
  112.8 5.8 %all_gather.25 = bf16[128,1024]{1,0:T(8,128)(2,1)S(1)} all-gather(bf16[128,256]{1,0:T(8,128)(2,1)S(1)} %convolution_convert_fusion.1), channel_id=1, replica_groups=mesh['fsdp'=8,'tp'=4] {'tp'}, dimensions={1}, use_global_device_ids=true | all-gather | bytes 327680 | tf_op jit(solution)/shard_map/all_gather | solution.py:53
  118.6 3.8 all-gather.9.cloned.1.call-done
  122.4 2.0 convolution_convert_fusion
  124.4 6.0 %all_gather.29 = bf16[128,1024]{1,0:T(8,128)(2,1)S(1)} all-gather(bf16[128,256]{1,0:T(8,128)(2,1)S(1)} %convolution_convert_fusion), channel_id=1, replica_groups=mesh['fsdp'=8,'tp'=4] {'tp'}, dimensions={1}, use_global_device_ids=true | all-gather | bytes 327680 | tf_op jit(solution)/shard_map/all_gather | solution.py:54
  130.4 104.2 %all-gather.7.cloned.1.call-done = bf16[1024,3584]{1,0:T(8,128)(2,1)} async-done(((bf16[128,3584]{1,0:T(8,128)(2,1)}), bf16[1024,3584]{1,0:T(8,128)(2,1)}) %all-gather.7.cloned.1.call-update) | async-done | bytes 7340048 | tf_op jit(solution)/shard_map/all_gather | solution.py:62
  234.6 5.5 %convolution_add_fusion.1 = f32[128,3584]{1,0:T(8,128)} fusion(f32[128,3584]{1,0:T(8,128)S(1)} %copy-done.7, bf16[128,1024]{1,0:T(8,128)(2,1)S(1)} %all_gather.25, bf16[1024,3584]{1,0:T(8,128)(2,1)} %all-gather.7.cloned.1.call-done), kind=kOutput, calls=%fused_computation.7 | convolution fusion | flops 939982848 | bytes 11272192 | tf_op jit(solution)/shard_map/dot_general | solution.py:72
  240.1 106.3 %all-gather.11.cloned.1.call-done = bf16[1024,3584]{1,0:T(8,128)(2,1)} async-done(((bf16[128,3584]{1,0:T(8,128)(2,1)}), bf16[1024,3584]{1,0:T(8,128)(2,1)}) %all-gather.11.cloned.1.call-update) | async-done | bytes 7340048 | tf_op jit(solution)/shard_map/all_gather | solution.py:63
  346.4 7.5 %fusion.2 = (bf16[128,3584]{1,0:T(8,128)(2,1)}, bf16[128,3584]{1,0:T(8,128)(2,1)}, bf16[128,3584]{1,0:T(8,128)(2,1)S(1)}) fusion(bf16[128,3584]{1,0:T(8,128)(2,1)} %param.23, f32[128,3584]{1,0:T(8,128)} %convolution_add_fusion.1, f32[128,3584]{1,0:T(8,128)} %copy.35, bf16[128,1024]{1,0:T(8,128)(2,1)S(1)} %all_gather.29, ...), kind=kOutput, calls=%fused_computation.12 | convolution fusion | flops 947322880 | bytes 14942208 | tf_op jit(solution)/shard_map/dot_general | solution.py:73
  353.9 1.3 copy.39
  355.1 1.7 copy.40
  356.8 0.7 gather_fusion.3
  357.5 0.5 fusion.9
  358.0 0.2 pad.5
  358.2 2.5 copy.47
  360.8 0.0 reduce-scatter.5.cloned.1.call-update
  360.8 0.0 reduce-scatter.3.cloned.1.call-start
  360.9 1.1 copy-done.8
  361.9 1.3 copy.36
  363.2 1.7 copy.37
  364.9 0.7 gather_fusion.2
  365.6 0.0 copy-done.4
  365.6 0.5 fusion.11
  366.1 0.2 pad.4
  366.3 2.5 copy.46
  368.8 0.0 reduce-scatter.3.cloned.1.call-update
  368.9 59.1 %reduce-scatter.5.cloned.1.call-done = f32[27,2048]{1,0:T(8,128)} async-done(((f32[27,16384]{1,0:T(8,128)}), f32[27,2048]{1,0:T(8,128)}) %reduce-scatter.5.cloned.1.call-update) | async-done | bytes 221200 | tf_op jit(solution)/shard_map/reduce_scatter | solution.py:85
  428.0 71.9 %reduce-scatter.3.cloned.1.call-done = f32[27,2048]{1,0:T(8,128)} async-done(((f32[27,16384]{1,0:T(8,128)}), f32[27,2048]{1,0:T(8,128)}) %reduce-scatter.3.cloned.1.call-update) | async-done | bytes 221200 | tf_op jit(solution)/shard_map/reduce_scatter | solution.py:84
  (27 shorter events, 0.1 us)
Async XLA Ops:
  7.2 2.9 copy-start
  7.2 103.6 %all-gather.5.cloned.1.call-start = ((), (), s32[]{:S(2)}) async-start(), calls=%async_computation.2 | async-start | bytes 2359296 | tf_op jit(solution)/shard_map/all_gather | solution.py:47
  7.9 114.5 %all-gather.9.cloned.1.call-start = ((), (), s32[]{:S(2)}) async-start(), calls=%async_computation.4 | async-start | bytes 2359296 | tf_op jit(solution)/shard_map/all_gather | solution.py:48
  8.7 226.0 %all-gather.7.cloned.1.call-start = ((), (), s32[]{:S(2)}) async-start(), calls=%async_computation.3 | async-start | bytes 8257536 | tf_op jit(solution)/shard_map/all_gather | solution.py:62
  9.4 337.0 %all-gather.11.cloned.1.call-start = ((), (), s32[]{:S(2)}) async-start(), calls=%async_computation.5 | async-start | bytes 8257536 | tf_op jit(solution)/shard_map/all_gather | solution.py:63
  10.0 418.0 %reduce-scatter.5.cloned.1.call-start = ((), (), s32[]{:S(2)}) async-start(), calls=%async_computation.7 | async-start | bytes 2359296 | tf_op jit(solution)/shard_map/reduce_scatter | solution.py:85
  10.0 1.4 copy-start.9
  11.4 38.4 %copy-start.1 = (bf16[128,32,128]{2,0,1:T(8,128)(2,1)}, bf16[128,32,128]{2,0,1:T(8,128)(2,1)S(1)}, u32[]{:S(2)}) copy-start(bf16[128,32,128]{2,0,1:T(8,128)(2,1)S(1)} %copy.30) | copy-start | bytes 3145732
  11.4 37.6 %copy-start.13 = (s32[27]{0:T(128)S(1)}, s32[27]{0:T(128)}, u32[]{:S(2)}) copy-start(s32[27]{0:T(128)} %param.16) | copy-start | bytes 328
  47.8 2.0 copy-start.11
  47.8 2.0 copy-start.12
  49.8 3.1 copy-start.3
  59.4 2.8 copy-start.14
  59.4 2.9 copy-start.2
  62.2 0.9 copy-start.10
  63.1 38.4 %copy-start.5 = (bf16[27,128,128]{2,1,0:T(8,128)(2,1)}, bf16[27,128,128]{2,1,0:T(8,128)(2,1)S(1)}, u32[]{:S(2)}) copy-start(bf16[27,128,128]{2,1,0:T(8,128)(2,1)S(1)} %gather_fusion.1) | copy-start | bytes 2654212
  118.6 116.1 %copy-start.7 = (f32[128,3584]{1,0:T(8,128)S(1)}, f32[128,3584]{1,0:T(8,128)}, u32[]{:S(2)}) copy-start(f32[128,3584]{1,0:T(8,128)} %copy.32) | copy-start | bytes 5505028
  355.1 2.4 copy-start.6
  360.8 1.2 copy-start.8
  360.8 139.1 %reduce-scatter.3.cloned.1.call-start = ((), (), s32[]{:S(2)}) async-start(), calls=%async_computation.6 | async-start | bytes 2359296 | tf_op jit(solution)/shard_map/reduce_scatter | solution.py:84
  363.2 2.4 copy-start.4
Sparse Core Ops, SparseCore 0:
  10.1 57.4 all-gather.4
  69.7 52.5 all-gather.8
  124.6 110.0 all-gather.6
  236.7 109.6 all-gather.10
  360.9 67.0 reduce-scatter.4
  431.9 67.9 reduce-scatter.2
where the time goes:
time: 507 us
  waiting for transfers between devices  348 us (69%)
  blocking collectives  84.6 us (17%)
  local copies, waits for them, and re-layouts  27.7 us (5%)
  matrix products  22.7 us (4%)
  between operations  14.4 us (3%)
  other arithmetic  9.16 us (2%)
    all_gather x1, waiting for transfers between devices, on_device(): right_up = lax.all_gather(up_right, 'fsdp', axis=0, tiled=True)  106 us
    all_gather x1, waiting for transfers between devices, on_device(): right_gate = lax.all_gather(gate_right, 'fsdp', axis=0, tiled=True)  104 us
    reduce_scatter x1, waiting for transfers between devices, on_device(): lax.psum_scatter(value_gate, 'fsdp', scatter_dimension=1, tiled=True)  71.9 us
    reduce_scatter x1, waiting for transfers between devices, on_device(): lax.psum_scatter(value_up, 'fsdp', scatter_dimension=1, tiled=True)  59.1 us
    all_gather x1, blocking collectives, on_device(): lax.all_gather(up_values, 'fsdp', axis=1, tiled=True)  36.5 us
    all_gather x1, blocking collectives, on_device(): lax.all_gather(gate_values, 'fsdp', axis=1, tiled=True)  36.4 us
  transfers between devices with their start and end apart: 6, of which 5 were waited for; matrix products, arithmetic and copies ran while one was open for 9% of the time, Pallas kernels for 0%

commit v1 on v0

--- a/solution.py
+++ b/solution.py
@@ -59,7 +59,12 @@
     )
     blocks_gate = flat_gate.reshape(flat_gate.shape[0], BLK, BLK)
     blocks_up = flat_up.reshape(flat_up.shape[0], BLK, BLK)
-    right_gate = lax.all_gather(gate_right, "fsdp", axis=0, tiled=True)
+    ring = [gate_right]
+    for hop in range(7):
+        ring.append(lax.ppermute(ring[-1], "fsdp", [(dev, (dev + 1) % 8) for dev in range(8)]))
+    right_gate = jnp.roll(
+        jnp.concatenate(ring[::-1], axis=0), (lax.axis_index("fsdp") + 1) * ring[0].shape[0], axis=0
+    )
     right_up = lax.all_gather(up_right, "fsdp", axis=0, tiled=True)
     col_blocks = right_gate.shape[1] // BLK
     col_base = lax.axis_index("tp") * col_blocks

time: 507 us -> 528 us (1.041)
  waiting for transfers between devices: 348 us -> 280 us
  blocking collectives: 84.6 us -> 145 us
  local copies, waits for them, and re-layouts: 27.7 us -> 55.3 us
    ppermute x0 -> x7, waiting for transfers between devices: none -> 144 us  [on_device(): lax.ppermute(ring[-1], 'fsdp', [(dev, (dev + 1) % 8) for dev in range(8)])]
    all_gather x1, waiting for transfers between devices: 106 us -> 0.01 us  [on_device(): right_up = lax.all_gather(up_right, 'fsdp', axis=0, tiled=True)]
    all_gather x1 -> x0, waiting for transfers between devices: 104 us -> none  [on_device(): right_gate = lax.all_gather(gate_right, 'fsdp', axis=0, tiled=True)]
    all_gather x1, blocking collectives: 36.5 us -> 67.1 us  [on_device(): lax.all_gather(up_values, 'fsdp', axis=1, tiled=True)]
    all_gather x1, blocking collectives: 36.4 us -> 66.1 us  [on_device(): lax.all_gather(gate_values, 'fsdp', axis=1, tiled=True)]
    unnamed x37 -> x68, local copies, waits for them, and re-layouts: 8.89 us -> 34.5 us
  transfers between devices with their start and end apart: 6 -> 12, of which waited for: 5 -> 7; matrix products, arithmetic and copies ran while one was open for 9% -> 12% of each run, Pallas kernels for 0% -> 0%
where the time goes in v1:
time: 528 us; the launch traced here: 527 us
  waiting for transfers between devices  280 us (53%)
  blocking collectives  145 us (27%)
  local copies, waits for them, and re-layouts  55.3 us (10%)
  matrix products  20.3 us (4%)
  between operations  14.1 us (3%)
  other arithmetic  9.16 us (2%)
    ppermute x7, waiting for transfers between devices, on_device(): lax.ppermute(ring[-1], 'fsdp', [(dev, (dev + 1) % 8) for dev in range(8)])  144 us
    reduce_scatter x1, waiting for transfers between devices, on_device(): lax.psum_scatter(value_gate, 'fsdp', scatter_dimension=1, tiled=True)  71.8 us
    all_gather x1, blocking collectives, on_device(): lax.all_gather(up_values, 'fsdp', axis=1, tiled=True)  67.1 us
    all_gather x1, blocking collectives, on_device(): lax.all_gather(gate_values, 'fsdp', axis=1, tiled=True)  66.1 us
    reduce_scatter x1, waiting for transfers between devices, on_device(): lax.psum_scatter(value_up, 'fsdp', scatter_dimension=1, tiled=True)  62 us
    unnamed x68, local copies, waits for them, and re-layouts  34.5 us
  transfers between devices with their start and end apart: 12, of which 7 were waited for; matrix products, arithmetic and copies ran while one was open for 12% of the time, Pallas kernels for 0%

profile of v1, /device:TPU:0, one launch (start us, length us, event | category | flops | bytes accessed | tf_op | source)
XLA Modules:
  0.0 527.1 jit_solution(484226704910111339)
XLA Ops:
  7.2 0.7 all-gather.6.cloned.1.call-update
  8.0 0.7 all-gather.4.cloned.1.call-update
  8.7 3.0 collective-permute-start
  11.7 32.0 %collective-permute-done = bf16[128,3584]{1,0:T(8,128)(2,1)S(1)} collective-permute-done((bf16[128,3584]{1,0:T(8,128)(2,1)}, bf16[128,3584]{1,0:T(8,128)(2,1)S(1)}, u32[]{:S(2)}, u32[]{:S(2)}) %collective-permute-start) | collective-permute-done | bytes 917536 | tf_op jit(solution)/shard_map/ppermute | solution.py:64
  43.8 40.3 %collective-permute-done.1 = bf16[128,3584]{1,0:T(8,128)(2,1)S(1)} collective-permute-done((bf16[128,3584]{1,0:T(8,128)(2,1)S(1)}, bf16[128,3584]{1,0:T(8,128)(2,1)S(1)}, u32[]{:S(2)}, u32[]{:S(2)}) %collective-permute-start.1) | collective-permute-done | bytes 917536 | tf_op jit(solution)/shard_map/ppermute | solution.py:64
  84.2 31.9 %collective-permute-done.2 = bf16[128,3584]{1,0:T(8,128)(2,1)S(1)} collective-permute-done((bf16[128,3584]{1,0:T(8,128)(2,1)S(1)}, bf16[128,3584]{1,0:T(8,128)(2,1)S(1)}, u32[]{:S(2)}, u32[]{:S(2)}) %collective-permute-start.2) | collective-permute-done | bytes 917536 | tf_op jit(solution)/shard_map/ppermute | solution.py:64
  116.1 0.9 copy-done.13
  117.0 39.9 %collective-permute-done.3 = bf16[128,3584]{1,0:T(8,128)(2,1)} collective-permute-done((bf16[128,3584]{1,0:T(8,128)(2,1)S(1)}, bf16[128,3584]{1,0:T(8,128)(2,1)}, u32[]{:S(2)}, u32[]{:S(2)}) %collective-permute-start.3) | collective-permute-done | bytes 917536 | tf_op jit(solution)/shard_map/ppermute | solution.py:64
  156.9 67.1 %all_gather.27 = bf16[27,16384]{1,0:T(8,128)(2,1)} all-gather(bf16[27,2048]{1,0:T(8,128)(2,1)} %param.20), channel_id=1, replica_groups=mesh['fsdp'=8,'tp'=4] {'fsdp'}, dimensions={1}, use_global_device_ids=true | all-gather | bytes 995328 | tf_op jit(solution)/shard_map/all_gather | solution.py:58
  224.0 1.3 copy.29
  225.3 1.7 copy.30
  227.1 2.9 copy.45
  230.0 0.7 gather_fusion.1
  230.8 3.1 fusion.10
  233.9 0.2 broadcast.16.clone
  234.1 4.6 scatter_fusion.1
  238.7 1.7 copy.34
  240.4 2.8 copy.35
  243.3 0.7 gather_fusion
  244.0 66.1 %all_gather.23 = bf16[27,16384]{1,0:T(8,128)(2,1)S(1)} all-gather(bf16[27,2048]{1,0:T(8,128)(2,1)S(1)} %copy-done.17), channel_id=1, replica_groups=mesh['fsdp'=8,'tp'=4] {'fsdp'}, dimensions={1}, use_global_device_ids=true | all-gather | bytes 995328 | tf_op jit(solution)/shard_map/all_gather | solution.py:57
  310.2 0.2 copy.44
  310.4 1.6 fusion.12
  312.1 0.2 broadcast.16.clone.1
  312.3 4.6 scatter_fusion
  316.8 1.7 copy.31
  318.6 2.8 copy.32
  321.4 2.0 convolution_convert_fusion
  323.4 5.9 %all_gather.25 = bf16[128,1024]{1,0:T(8,128)(2,1)S(1)} all-gather(bf16[128,256]{1,0:T(8,128)(2,1)S(1)} %convolution_convert_fusion), channel_id=1, replica_groups=mesh['fsdp'=8,'tp'=4] {'tp'}, dimensions={1}, use_global_device_ids=true | all-gather | bytes 327680 | tf_op jit(solution)/shard_map/all_gather | solution.py:54
  329.3 2.0 convolution_convert_fusion.1
  331.4 6.0 %all_gather.22 = bf16[128,1024]{1,0:T(8,128)(2,1)S(1)} all-gather(bf16[128,256]{1,0:T(8,128)(2,1)S(1)} %convolution_convert_fusion.1), channel_id=1, replica_groups=mesh['fsdp'=8,'tp'=4] {'tp'}, dimensions={1}, use_global_device_ids=true | all-gather | bytes 327680 | tf_op jit(solution)/shard_map/all_gather | solution.py:53
  337.4 0.2 collective-permute-done.6
  337.6 1.0 constant_dynamic-update-slice_fusion.15
  338.6 2.2 constant_dynamic-update-slice_fusion.14
  340.8 2.2 constant_dynamic-update-slice_fusion.13
  343.1 2.3 constant_dynamic-update-slice_fusion.12
  345.3 1.0 constant_dynamic-update-slice_fusion.11
  346.3 1.0 constant_dynamic-update-slice_fusion.10
  347.4 1.0 constant_dynamic-update-slice_fusion.9
  348.4 1.0 constant_dynamic-update-slice_fusion.8
  349.4 1.1 constant_dynamic-update-slice_fusion.7
  350.5 2.3 constant_dynamic-update-slice_fusion.6
  352.7 2.1 constant_dynamic-update-slice_fusion.5
  354.9 2.2 constant_dynamic-update-slice_fusion.4
  357.0 1.0 constant_dynamic-update-slice_fusion.3
  358.0 1.0 constant_dynamic-update-slice_fusion.2
  359.1 1.0 constant_dynamic-update-slice_fusion.1
  360.1 1.0 constant_dynamic-update-slice_fusion
  361.1 4.4 convolution_add_fusion
  365.5 6.2 %fusion.7 = (bf16[128,3584]{1,0:T(8,128)(2,1)}, bf16[128,3584]{1,0:T(8,128)(2,1)}, bf16[128,3584]{1,0:T(8,128)(2,1)S(1)}) fusion(f32[128,3584]{1,0:T(8,128)S(1)} %convolution_add_fusion, bf16[128,3584]{1,0:T(8,128)(2,1)S(1)} %copy-done.20, f32[128,3584]{1,0:T(8,128)S(1)} %copy-done.15, bf16[128,1024]{1,0:T(8,128)(2,1)S(1)} %all_gather.22, ...), kind=kOutput, calls=%fused_computation.14 | convolution fusion | flops 947322880 | bytes 14942212 | tf_op jit(solution)/shard_map/dot_general | solution.py:77
  371.7 1.3 copy.39
  373.0 1.7 copy.40
  374.6 0.7 gather_fusion.3
  375.4 0.5 fusion.14
  375.8 0.2 pad.5
  376.1 2.6 copy.47
  378.7 1.1 copy-done.16
  379.8 1.3 copy.36
  381.1 1.7 copy.37
  382.7 0.7 gather_fusion.2
  383.5 0.5 fusion.16
  383.9 0.2 pad.4
  384.2 2.5 copy.46
  386.7 62.0 %reduce-scatter.5.cloned.1.call-done = f32[27,2048]{1,0:T(8,128)} async-done(((f32[27,16384]{1,0:T(8,128)}), f32[27,2048]{1,0:T(8,128)}) %reduce-scatter.5.cloned.1.call-update) | async-done | bytes 221200 | tf_op jit(solution)/shard_map/reduce_scatter | solution.py:90
  448.7 71.8 %reduce-scatter.3.cloned.1.call-done = f32[27,2048]{1,0:T(8,128)} async-done(((f32[27,16384]{1,0:T(8,128)}), f32[27,2048]{1,0:T(8,128)}) %reduce-scatter.3.cloned.1.call-update) | async-done | bytes 221200 | tf_op jit(solution)/shard_map/reduce_scatter | solution.py:89
  (70 shorter events, 0.4 us)
Async XLA Ops:
  7.2 216.9 %copy-start = (bf16[128,4096]{1,0:T(8,128)(2,1)S(1)}, bf16[128,4096]{1,0:T(8,128)(2,1)}, u32[]{:S(2)}) copy-start(bf16[128,4096]{1,0:T(8,128)(2,1)} %param.12) | copy-start | bytes 3145732
  7.2 314.2 %all-gather.6.cloned.1.call-start = ((), (), s32[]{:S(2)}) async-start(), calls=%async_computation.3 | async-start | bytes 2359296 | tf_op jit(solution)/shard_map/all_gather | solution.py:48
  7.9 321.4 %all-gather.4.cloned.1.call-start = ((), (), s32[]{:S(2)}) async-start(), calls=%async_computation.2 | async-start | bytes 2359296 | tf_op jit(solution)/shard_map/all_gather | solution.py:47
  8.7 352.4 %all-gather.8.cloned.1.call-start = ((), (), s32[]{:S(2)}) async-start(), calls=%async_computation.4 | async-start | bytes 8257536 | tf_op jit(solution)/shard_map/all_gather | solution.py:68
  8.7 35.1 %collective-permute-start = (bf16[128,3584]{1,0:T(8,128)(2,1)}, bf16[128,3584]{1,0:T(8,128)(2,1)S(1)}, u32[]{:S(2)}, u32[]{:S(2)}) collective-permute-start(bf16[128,3584]{1,0:T(8,128)(2,1)} %param.14), channel_id=1, source_target_pairs={{0,4},{4,8},{8,12},{12,16},{16,20},{20,24},{24,28},{28,0},{1,5},{5... | collective-permute-start | bytes 2752520 | tf_op jit(solution)/shard_map/ppermute | solution.py:64
  43.8 181.6 %copy-start.9 = (bf16[128,3584]{1,0:T(8,128)(2,1)}, bf16[128,3584]{1,0:T(8,128)(2,1)S(1)}, u32[]{:S(2)}) copy-start(bf16[128,3584]{1,0:T(8,128)(2,1)S(1)} %collective-permute-done) | copy-start | bytes 2752516
  43.8 40.4 %collective-permute-start.1 = (bf16[128,3584]{1,0:T(8,128)(2,1)S(1)}, bf16[128,3584]{1,0:T(8,128)(2,1)S(1)}, u32[]{:S(2)}, u32[]{:S(2)}) collective-permute-start(bf16[128,3584]{1,0:T(8,128)(2,1)S(1)} %collective-permute-done), channel_id=1, source_target_pairs={{0,4},{4,8},{8,12},{12,16},{16,20},{20,24},{24,28},{28,0},{1,5},{5... | collective-permute-start | bytes 2752520 | tf_op jit(solution)/shard_map/ppermute | solution.py:64
  43.8 404.9 %reduce-scatter.5.cloned.1.call-start = ((), (), s32[]{:S(2)}) async-start(), calls=%async_computation.6 | async-start | bytes 2359296 | tf_op jit(solution)/shard_map/reduce_scatter | solution.py:90
  84.2 141.1 %copy-start.11 = (bf16[128,3584]{1,0:T(8,128)(2,1)}, bf16[128,3584]{1,0:T(8,128)(2,1)S(1)}, u32[]{:S(2)}) copy-start(bf16[128,3584]{1,0:T(8,128)(2,1)S(1)} %collective-permute-done.1) | copy-start | bytes 2752516
  84.2 31.9 %collective-permute-start.2 = (bf16[128,3584]{1,0:T(8,128)(2,1)S(1)}, bf16[128,3584]{1,0:T(8,128)(2,1)S(1)}, u32[]{:S(2)}, u32[]{:S(2)}) collective-permute-start(bf16[128,3584]{1,0:T(8,128)(2,1)S(1)} %collective-permute-done.1), channel_id=1, source_target_pairs={{0,4},{4,8},{8,12},{12,16},{16,20},{20,24},{24,28},{28,0},{1,5},{5... | collective-permute-start | bytes 2752520 | tf_op jit(solution)/shard_map/ppermute | solution.py:64
  116.1 0.9 copy-start.13
  117.0 39.9 %collective-permute-start.3 = (bf16[128,3584]{1,0:T(8,128)(2,1)S(1)}, bf16[128,3584]{1,0:T(8,128)(2,1)}, u32[]{:S(2)}, u32[]{:S(2)}) collective-permute-start(bf16[128,3584]{1,0:T(8,128)(2,1)S(1)} %collective-permute-done.2), channel_id=1, source_target_pairs={{0,4},{4,8},{8,12},{12,16},{16,20},{20,24},{24,28},{28,0},{1,5},{5... | collective-permute-start | bytes 2752520 | tf_op jit(solution)/shard_map/ppermute | solution.py:64
  156.9 77.0 %collective-permute-start.4 = (bf16[128,3584]{1,0:T(8,128)(2,1)}, bf16[128,3584]{1,0:T(8,128)(2,1)}, u32[]{:S(2)}, u32[]{:S(2)}) collective-permute-start(bf16[128,3584]{1,0:T(8,128)(2,1)} %collective-permute-done.3), channel_id=1, source_target_pairs={{0,4},{4,8},{8,12},{12,16},{16,20},{20,24},{24,28},{28,0},{1,5},{5... | collective-permute-start | bytes 2752520 | tf_op jit(solution)/shard_map/ppermute | solution.py:64
  225.3 4.6 copy-start.21
  227.0 3.7 copy-start.1
  227.0 3.7 copy-start.18
  227.0 3.7 copy-start.19
  230.7 3.2 copy-start.3
  230.7 3.2 copy-start.22
  233.9 87.4 %collective-permute-start.5 = (bf16[128,3584]{1,0:T(8,128)(2,1)}, bf16[128,3584]{1,0:T(8,128)(2,1)}, u32[]{:S(2)}, u32[]{:S(2)}) collective-permute-start(bf16[128,3584]{1,0:T(8,128)(2,1)} %collective-permute-done.4), channel_id=1, source_target_pairs={{0,4},{4,8},{8,12},{12,16},{16,20},{20,24},{24,28},{28,0},{1,5},{5... | collective-permute-start | bytes 2752520 | tf_op jit(solution)/shard_map/ppermute | solution.py:64
  240.4 2.9 copy-start.2
  240.4 3.6 copy-start.17
  244.0 68.0 %copy-start.5 = (bf16[27,128,128]{2,1,0:T(8,128)(2,1)}, bf16[27,128,128]{2,1,0:T(8,128)(2,1)S(1)}, u32[]{:S(2)}) copy-start(bf16[27,128,128]{2,1,0:T(8,128)(2,1)S(1)} %gather_fusion) | copy-start | bytes 2654212
  321.3 16.3 %collective-permute-start.6 = (bf16[128,3584]{1,0:T(8,128)(2,1)}, bf16[128,3584]{1,0:T(8,128)(2,1)S(1)}, u32[]{:S(2)}, u32[]{:S(2)}) collective-permute-start(bf16[128,3584]{1,0:T(8,128)(2,1)} %collective-permute-done.5), channel_id=1, source_target_pairs={{0,4},{4,8},{8,12},{12,16},{16,20},{20,24},{24,28},{28,0},{1,5},{5... | collective-permute-start | bytes 2752520 | tf_op jit(solution)/shard_map/ppermute | solution.py:64
  340.8 4.5 copy-start.14
  343.1 3.3 copy-start.12
  345.3 2.0 copy-start.10
  346.3 2.0 copy-start.8
  359.1 2.0 copy-start.7
  361.1 4.4 copy-start.15
  361.1 4.4 copy-start.20
  373.0 2.4 copy-start.4
  378.6 1.2 copy-start.16
  378.7 141.9 %reduce-scatter.3.cloned.1.call-start = ((), (), s32[]{:S(2)}) async-start(), calls=%async_computation.5 | async-start | bytes 2359296 | tf_op jit(solution)/shard_map/reduce_scatter | solution.py:89
  381.1 2.4 copy-start.6
Sparse Core Ops, SparseCore 0:
  10.1 70.4 all-gather.5
  82.7 70.8 all-gather.3
  155.8 165.0 all-gather.7
  378.8 69.9 reduce-scatter.4
  452.7 67.7 reduce-scatter.2
